TPU v7x, 512 devices: a whole 4x8x8 slice. The times are simulated.
512 devices in a mesh: expert: 128 (over y, z, core), dp: 4 (over x).
Axes of the slice: x: 4, y: 8, z: 8, core: 2. Of those that a mesh axis runs over, the one named last changes fastest.
Arguments:
- hidden: bfloat16 [128, 4, 256, 1024], P('expert', 'dp'), may hold values from -6 to 6
- w_down: bfloat16 [128, 1024, 3584], P('expert', 'dp'), may hold values from -0.1875 to 0.1875
- expert_ids: int32 [4, 2048, 8], P('dp', 'expert'), may hold values from 0 to 127, all different within a row; in each aligned block of 16 rows (0 to 15, 16 to 31, ..., all dimensions but the last counted through in order) at most 2 rows name the same one
- route_weights: float32 [4, 2048, 8], P('dp', 'expert'), may hold values from 0.1 to 0.6
- grad_out: bfloat16 [4, 2048, 3584], P('dp', 'expert'), may hold values from -6 to 6
Outputs:
- mixed: bfloat16 [4, 2048, 3584], P('dp', 'expert')
- d_hidden: bfloat16 [128, 4, 256, 1024], P('expert', 'dp')
- d_w_down: bfloat16 [128, 1024, 3584], P('expert', 'dp')
- d_route: float32 [4, 2048, 8], P('dp', 'expert')
Inputs may be any that keep to these rules, and one draw needn't show every extreme that they name: `expert_ids`: among the 16 tokens of one device no expert is chosen more than 2 times, and some expert is chosen exactly 2 times; the 8 choices of a token are distinct.
All inputs are finite; a program needn't handle non-finite values.
Results may differ from a plain program's by a relative error of at most 0.0085.
Values may be sent and summed in bfloat16 or wider, within the bound.
A program may use at most 128 MiB of HBM per device.

v0:
```python
import jax
import jax.numpy as jnp
from jax import lax
from jax.sharding import PartitionSpec as P


def slot_ranks(choices, experts):
    flat = choices.reshape(-1)
    onehot = (flat[:, None] == jnp.arange(experts, dtype=jnp.int32)[None, :]).astype(jnp.int32)
    earlier = jnp.cumsum(onehot, axis=0) - onehot
    return jnp.sum(earlier * onehot, axis=1).reshape(choices.shape)


def on_device(hidden, w_down, expert_ids, route_weights, grad_out):
    experts = lax.axis_size("expert")
    groups = lax.axis_size("dp")
    slots = hidden.shape[2] // experts
    width = w_down.shape[2]
    w_whole = lax.all_gather(w_down, "dp", axis=1, tiled=True)[0]
    out_slots = jnp.dot(hidden[0, 0], w_whole, preferred_element_type=jnp.float32).astype(
        jnp.bfloat16
    )
    arrived = lax.all_to_all(
        out_slots.reshape(experts, slots, width), "expert", split_axis=0, concat_axis=0, tiled=True
    )
    arrived = arrived.reshape(experts * slots, width)
    choices = expert_ids[0]
    weights = route_weights[0]
    cotangent = grad_out[0].astype(jnp.float32)
    rows = choices * slots + slot_ranks(choices, experts)
    out_pair = arrived[rows].astype(jnp.float32)
    mixed = jnp.einsum("tk,tkd->td", weights, out_pair)
    d_route = jnp.einsum("td,tkd->tk", cotangent, out_pair)
    grad_pair = (weights[..., None] * cotangent[:, None, :]).astype(jnp.bfloat16)
    outgoing = jnp.zeros((experts * slots, width), jnp.bfloat16)
    outgoing = outgoing.at[rows.reshape(-1)].set(grad_pair.reshape(-1, width))
    mine = lax.all_to_all(
        outgoing.reshape(experts, 1, slots, width),
        "expert",
        split_axis=0,
        concat_axis=0,
        tiled=True,
    )
    own_grads = mine[:, 0]
    d_hidden = jnp.einsum(
        "rd,hd->rh", own_grads.reshape(-1, width), w_whole, preferred_element_type=jnp.float32
    ).astype(jnp.bfloat16)
    columns = lax.all_to_all(hidden, "dp", split_axis=3, concat_axis=1, tiled=True)[0]
    columns = columns.reshape(groups, experts, slots, columns.shape[-1])
    cw = width // 2
    parts = []
    for c in range(2):
        slot_grads = lax.all_gather(mine[..., c * cw : (c + 1) * cw], "dp", axis=1, tiled=True)
        parts.append(
            jnp.einsum(
                "gsch,sgcd->hd", columns, slot_grads, preferred_element_type=jnp.float32
            ).astype(jnp.bfloat16)
        )
    d_weight = jnp.concatenate(parts, axis=1)
    return (
        mixed.astype(jnp.bfloat16)[None],
        d_hidden.reshape(hidden.shape),
        d_weight[None],
        d_route[None],
    )


def solution(mesh):
    placed = (
        P("expert", "dp", None, None),
        P("expert", "dp", None),
        P("dp", "expert", None),
        P("dp", "expert", None),
        P("dp", "expert", None),
    )
    return jax.shard_map(
        on_device,
        mesh=mesh,
        in_specs=placed,
        out_specs=(
            P("dp", "expert", None),
            P("expert", "dp", None, None),
            P("expert", "dp", None),
            P("dp", "expert", None),
        ),
        check_vma=False,
    )
```

profile of v0, /device:TPU:1, one launch (start us, length us, event | category | flops | bytes accessed | tf_op | source)
XLA Modules:
  0.0 227.6 jit_solution(7683013739206800182)
XLA Ops:
  7.2 0.7 all-gather.4.cloned.1.call-update
  9.0 2.5 %scatter_custom_fusion = bf16[256,3584]{1,0:T(8,128)(2,1)S(1)} fusion(s32[128]{0:T(128)S(1)} %fusion.33, f32[16,3584]{1,0:T(8,128)S(1)} %bitcast_convert_fusion.1, f32[128]{0:T(128)S(1)} %mul.53, bf16[]{:T(256)} %constant.7.clone.1), kind=kCustom, calls=%fused_computation.18 | custom fusion | flops 917504 | bytes 2064898 | tf_op jit(solution)/shard_map/scatter | solution.py:36
  11.5 1.6 reshape.99
  13.2 64.9 %all_to_all.25 = bf16[128,1,2,3584]{3,2,1,0:T(2,128)(2,1)S(1)} all-to-all(bf16[128,1,2,3584]{3,2,1,0:T(2,128)(2,1)} %bitcast.87), channel_id=1, replica_groups=mesh['expert'=128,'dp'=4] {'expert'}, dimensions={0} | all-to-all | bytes 3670016 | tf_op jit(solution)/shard_map/all_to_all | solution.py:37
  78.1 2.2 fusion.34
  80.2 3.6 %copy.71 = bf16[128,1,2,1792]{0,3,1,2:T(8,128)(2,1)} copy(bf16[128,1,2,1792]{3,2,1,0:T(2,128)(2,1)} %get-tuple-element.24) | data formatting | bytes 1835008
  83.9 2.1 copy.72
  86.0 0.9 copy.58
  87.4 3.8 %reduce = bf16[1024,256]{1,0:T(8,128)(2,1)S(1)} reduce(bf16[1024,1,1,256]{3,2,1,0:T(2,128)(2,1)S(1)} %bitcast.89, bf16[]{:T(256)} %broadcast.58), dimensions={1,2}, to_apply=%bitcast.78.reduce_sub_computation | reduce | bytes 1048578
  91.3 0.9 reshape.126
  92.2 4.0 %all-to-all-start.2 = ((bf16[4,2,32768]{2,1,0:T(2,128)(2,1)}), bf16[4,2,32768]{2,1,0:T(2,128)(2,1)S(1)}, u32[]{:S(2)}, u32[]{:S(2)}) async-start(bf16[4,2,32768]{2,1,0:T(2,128)(2,1)} %reshape.126), calls=%async_computation.2 | async-start | bytes 1048576 | tf_op jit(solution)/shard_map/all_to_all | solution.py:48
  96.2 6.4 %fusion.4 = bf16[256,3584]{1,0:T(8,128)(2,1)} fusion(bf16[1,1024,3584]{2,1,0:T(8,128)(2,1)} %all-gather.4.cloned.1.call-done, bf16[1,1,256,1024]{3,2,1,0:T(8,128)(2,1)S(1)} %copy-done.1), kind=kOutput, calls=%fused_computation.6 | convolution fusion | flops 1879965696 | bytes 9699328 | tf_op jit(solution)/shard_map/dot_general | solution.py:20
  102.6 4.8 %reshape.96 = bf16[128,2,3584]{2,1,0:T(2,128)(2,1)} reshape(bf16[256,3584]{1,0:T(8,128)(2,1)} %fusion.4) | data formatting | bytes 3670016 | tf_op jit(solution)/shard_map/reshape | solution.py:24
  107.3 15.9 %all-to-all-start = ((bf16[128,2,3584]{2,1,0:T(2,128)(2,1)}), bf16[128,2,3584]{2,1,0:T(2,128)(2,1)}, u32[]{:S(2)}, u32[]{:S(2)}) async-start(bf16[128,2,3584]{2,1,0:T(2,128)(2,1)} %reshape.96), calls=%async_computation | async-start | bytes 3670016 | tf_op jit(solution)/shard_map/all_to_all | solution.py:23
  124.3 1.1 copy.59
  125.3 1.7 reshape_squeeze.6
  127.0 22.5 %all-gather.6.cloned.1.call-done = bf16[128,4,2,1792]{0,3,1,2:T(8,128)(2,1)} async-done(((bf16[128,1,2,1792]{0,3,1,2:T(8,128)(2,1)}), bf16[128,4,2,1792]{0,3,1,2:T(8,128)(2,1)}) %all-gather.6.cloned.1.call-update) | async-done | bytes 3670032 | tf_op jit(solution)/shard_map/all_gather | solution.py:53
  149.5 3.2 %fusion.10 = bf16[256,1792]{0,1:T(8,128)(2,1)S(1)} fusion(bf16[128,4,2,1792]{0,3,1,2:T(8,128)(2,1)} %all-gather.6.cloned.1.call-done, bf16[4,128,2,256]{3,0,2,1:T(4,128)(2,1)S(1)} %bitcast.91), kind=kOutput, calls=%fused_computation.12 | convolution fusion | flops 939982848 | bytes 5111808 | tf_op jit(solution)/shard_map/gsch,sgcd->hd/dot_general | solution.py:55
  152.7 48.4 %all-gather.8.cloned.1.call-done = bf16[128,4,2,1792]{0,3,1,2:T(8,128)(2,1)} async-done(((bf16[128,1,2,1792]{0,3,1,2:T(8,128)(2,1)}), bf16[128,4,2,1792]{0,3,1,2:T(8,128)(2,1)}) %all-gather.8.cloned.1.call-update) | async-done | bytes 3670032 | tf_op jit(solution)/shard_map/all_gather | solution.py:53
  201.1 3.2 %fusion.9 = bf16[256,1792]{0,1:T(8,128)(2,1)S(1)} fusion(bf16[128,4,2,1792]{0,3,1,2:T(8,128)(2,1)} %all-gather.8.cloned.1.call-done, bf16[4,128,2,256]{3,0,2,1:T(4,128)(2,1)S(1)} %bitcast.92), kind=kOutput, calls=%fused_computation.11 | convolution fusion | flops 939982848 | bytes 5111808 | tf_op jit(solution)/shard_map/gsch,sgcd->hd/dot_general | solution.py:55
  204.4 2.6 %copy.63 = bf16[1,256,3584]{2,1,0:T(8,128)(2,1)} copy(bf16[1,256,3584]{1,2,0:T(8,128)(2,1)S(1)} %maximum_bitcast_fusion) | data formatting | bytes 3670016
  207.0 6.5 %fusion.15 = bf16[1,1,256,1024]{3,2,1,0:T(8,128)(2,1)} fusion(bf16[256,3584]{1,0:T(8,128)(2,1)} %reshape_squeeze.6, bf16[1,1024,3584]{2,1,0:T(8,128)(2,1)} %all-gather.4.cloned.1.call-done), kind=kOutput, calls=%fused_computation.17 | convolution fusion | flops 1879310336 | bytes 9699328 | tf_op jit(solution)/shard_map/rd,hd->rh/dot_general | solution.py:45
  213.5 4.1 %reshape.97 = bf16[256,3584]{1,0:T(8,128)(2,1)S(1)} reshape(bf16[128,2,3584]{2,1,0:T(2,128)(2,1)} %all-to-all-done) | data formatting | bytes 3670016 | tf_op jit(solution)/shard_map/reshape | solution.py:26
  217.6 1.1 gather_fusion
  (47 shorter events, 5.1 us)
Async XLA Ops:
  7.2 0.8 copy-start.4
  7.2 1.1 copy-start.5
  7.2 1.8 copy-start.3
  7.2 89.0 %all-gather.4.cloned.1.call-start = ((), (), s32[]{:S(2)}) async-start(), calls=%async_computation.3 | async-start | bytes 9175040 | tf_op jit(solution)/shard_map/all_gather | solution.py:19
  7.9 141.6 %all-gather.6.cloned.1.call-start = ((), (), s32[]{:S(2)}) async-start(), calls=%async_computation.4 | async-start | bytes 4587520 | tf_op jit(solution)/shard_map/all_gather | solution.py:53
  83.8 2.2 copy-start
  83.8 117.3 %all-gather.8.cloned.1.call-start = ((), (), s32[]{:S(2)}) async-start(), calls=%async_computation.5 | async-start | bytes 4587520 | tf_op jit(solution)/shard_map/all_gather | solution.py:53
  91.3 4.9 %copy-start.1 = (bf16[1,1,256,1024]{3,2,1,0:T(8,128)(2,1)S(1)}, bf16[1,1,256,1024]{3,2,1,0:T(8,128)(2,1)}, u32[]{:S(2)}) copy-start(bf16[1,1,256,1024]{3,2,1,0:T(8,128)(2,1)} %param.5) | copy-start | bytes 1572868
  92.2 15.2 %all-to-all-start.2 = ((bf16[4,2,32768]{2,1,0:T(2,128)(2,1)}), bf16[4,2,32768]{2,1,0:T(2,128)(2,1)S(1)}, u32[]{:S(2)}, u32[]{:S(2)}) async-start(bf16[4,2,32768]{2,1,0:T(2,128)(2,1)} %reshape.126), calls=%async_computation.2 | async-start | bytes 1048576 | tf_op jit(solution)/shard_map/all_to_all | solution.py:48
  107.3 106.2 %all-to-all-start = ((bf16[128,2,3584]{2,1,0:T(2,128)(2,1)}), bf16[128,2,3584]{2,1,0:T(2,128)(2,1)}, u32[]{:S(2)}, u32[]{:S(2)}) async-start(bf16[128,2,3584]{2,1,0:T(2,128)(2,1)} %reshape.96), calls=%async_computation | async-start | bytes 3670016 | tf_op jit(solution)/shard_map/all_to_all | solution.py:23
  125.3 24.2 %copy-start.2 = (bf16[1,4,1,256,256]{4,1,3,2,0:T(4,128)(2,1)S(1)}, bf16[1,4,1,256,256]{4,1,3,2,0:T(4,128)(2,1)}, u32[]{:S(2)}) copy-start(bf16[1,4,1,256,256]{4,1,3,2,0:T(4,128)(2,1)} %copy.59) | copy-start | bytes 1572868
Sparse Core Ops, SparseCore 0:
  10.1 84.9 all-gather.3
  97.2 52.2 all-gather.5
  151.6 49.4 all-gather.7
where the time goes:
time: 228 us
  waiting for transfers between devices  71.7 us (31%)
  blocking collectives  64.9 us (28%)
  local copies, waits for them, and re-layouts  29.9 us (13%)
  matrix products  20.3 us (9%)
  starting transfers between devices  20 us (9%)
  between operations  14 us (6%)
  other arithmetic  6.95 us (3%)
    all_gather x2, waiting for transfers between devices, on_device(): lax.all_gather(mine[..., c * cw:(c + 1) * cw], 'dp', axis=1, tiled=True)  70.9 us
    all_to_all x1, blocking collectives, on_device(): lax.all_to_all(outgoing.reshape(experts, 1, slots, width), 'expert', spli...  64.9 us
    all_to_all x1, starting transfers between devices, on_device(): lax.all_to_all(out_slots.reshape(experts, slots, width), 'expert', split_...  15.9 us
    unnamed x22, local copies, waits for them, and re-layouts  11.3 us
    dot_general x1, matrix products, on_device(): jnp.einsum('rd,hd->rh', own_grads.reshape(-1, width), w_whole, preferred_...  6.53 us
    dot_general x1, matrix products, on_device(): jnp.dot(hidden[0, 0], w_whole, preferred_element_type=jnp.float32)  6.37 us
    dot_general x2, matrix products, on_device(): jnp.einsum('gsch,sgcd->hd', columns, slot_grads, preferred_element_type=j...  6.36 us
    reshape x1, local copies, waits for them, and re-layouts, on_device(): out_slots.reshape(experts, slots, width)  4.77 us
  transfers between devices with their start and end apart: 5, of which 2 were waited for; matrix products, arithmetic and copies ran while one was open for 22% of the time, Pallas kernels for 0%

commit v1 on v0

--- a/solution.py
+++ b/solution.py
@@ -50,7 +50,12 @@
     cw = width // 2
     parts = []
     for c in range(2):
-        slot_grads = lax.all_gather(mine[..., c * cw : (c + 1) * cw], "dp", axis=1, tiled=True)
+        slot_grads = jnp.concatenate(
+            lax.all_to_all(
+                jnp.stack([mine[..., c * cw : (c + 1) * cw]] * lax.axis_size("dp")), "dp", 0, 0
+            ),
+            axis=1,
+        )
         parts.append(
             jnp.einsum(
                 "gsch,sgcd->hd", columns, slot_grads, preferred_element_type=jnp.float32

time: 228 us -> 270 us (1.18)
  waiting for transfers between devices: 71.7 us -> 145 us
  blocking collectives: 64.9 us -> 0 us
  starting transfers between devices: 20 us -> 46.6 us
  local copies, waits for them, and re-layouts: 29.9 us -> 36.1 us
    all_to_all x0 -> x3, waiting for transfers between devices: none -> 108 us  [the longest x2 67.4 us: on_device(): lax.all_to_all(jnp.stack([mine[..., c * cw:(c + 1) * cw]] * lax.axis_size...]
    all_gather x2 -> x0, waiting for transfers between devices: 70.9 us -> none  [on_device(): lax.all_gather(mine[..., c * cw:(c + 1) * cw], 'dp', axis=1, tiled=True)]
    all_to_all x1 -> x0, blocking collectives: 64.9 us -> none  [on_device(): lax.all_to_all(outgoing.reshape(experts, 1, slots, width), 'expert', spli...]
    all_to_all x0 -> x3, starting transfers between devices: none -> 28.3 us  [the longest x1 18.5 us: on_device(): lax.all_to_all(outgoing.reshape(experts, 1, slots, width), 'expert', spli...]
    all_to_all x1, waiting for transfers between devices: 0.01 us -> 27.6 us  [on_device(): lax.all_to_all(out_slots.reshape(experts, slots, width), 'expert', split_...]
    all_to_all x1, waiting for transfers between devices: 0.01 us -> 9.34 us  [on_device(): lax.all_to_all(hidden, 'dp', split_axis=3, concat_axis=1, tiled=True)[0]]
    another operation x0 -> x2, local copies, waits for them, and re-layouts: none -> 6.98 us  [on_device(): jnp.stack([mine[..., c * cw:(c + 1) * cw]] * lax.axis_size('dp'))]
    slice x1 -> x3, local copies, waits for them, and re-layouts: 2.18 us -> 7.9 us  [on_device(): mine[..., c * cw:(c + 1) * cw]]
  transfers between devices with their start and end apart: 5 -> 6, of which waited for: 2 -> 5; matrix products, arithmetic and copies ran while one was open for 22% -> 21% of each run, Pallas kernels for 0% -> 0%
where the time goes in v1:
time: 270 us
  waiting for transfers between devices  145 us (54%)
  starting transfers between devices  46.6 us (17%)
  local copies, waits for them, and re-layouts  36.1 us (13%)
  matrix products  20.3 us (8%)
  between operations  14.3 us (5%)
  other arithmetic  6.96 us (3%)
    all_to_all x2, waiting for transfers between devices, on_device(): lax.all_to_all(jnp.stack([mine[..., c * cw:(c + 1) * cw]] * lax.axis_size...  67.4 us
    all_to_all x1, waiting for transfers between devices, on_device(): lax.all_to_all(outgoing.reshape(experts, 1, slots, width), 'expert', spli...  40.3 us
    all_to_all x1, waiting for transfers between devices, on_device(): lax.all_to_all(out_slots.reshape(experts, slots, width), 'expert', split_...  27.6 us
    all_to_all x1, starting transfers between devices, on_device(): lax.all_to_all(outgoing.reshape(experts, 1, slots, width), 'expert', spli...  18.5 us
    all_to_all x1, starting transfers between devices, on_device(): lax.all_to_all(out_slots.reshape(experts, slots, width), 'expert', split_...  14.3 us
    all_to_all x2, starting transfers between devices, on_device(): lax.all_to_all(jnp.stack([mine[..., c * cw:(c + 1) * cw]] * lax.axis_size...  9.81 us
    all_to_all x1, waiting for transfers between devices, on_device(): lax.all_to_all(hidden, 'dp', split_axis=3, concat_axis=1, tiled=True)[0]  9.34 us
    slice x3, local copies, waits for them, and re-layouts, on_device(): mine[..., c * cw:(c + 1) * cw]  7.9 us
  transfers between devices with their start and end apart: 6, of which 5 were waited for; matrix products, arithmetic and copies ran while one was open for 21% of the time, Pallas kernels for 0%

profile of v1, /device:TPU:1, one launch (start us, length us, event | category | flops | bytes accessed | tf_op | source)
XLA Modules:
  0.0 269.6 jit_solution(16284196985000452039)
XLA Ops:
  8.9 2.5 scatter_custom_fusion
  13.1 18.5 %all-to-all-start.1 = ((bf16[128,1,2,3584]{3,2,1,0:T(2,128)(2,1)}), bf16[128,1,2,3584]{3,2,1,0:T(2,128)(2,1)S(1)}, u32[]{:S(2)}, u32[]{:S(2)}) async-start(bf16[128,1,2,3584]{3,2,1,0:T(2,128)(2,1)} %bitcast.111), calls=%async_computation.1 | async-start | bytes 3670016 | tf_op jit(solution)/shard_map/all_to_all | solution.py:37
  33.1 3.8 %reduce = bf16[1024,256]{1,0:T(8,128)(2,1)S(1)} reduce(bf16[1024,1,1,256]{3,2,1,0:T(2,128)(2,1)S(1)} %bitcast.113, bf16[]{:T(256)} %broadcast.64), dimensions={1,2}, to_apply=%bitcast.104.reduce_sub_computation | reduce | bytes 1048578
  37.8 40.3 %all-to-all-done.1 = bf16[128,1,2,3584]{3,2,1,0:T(2,128)(2,1)S(1)} async-done(((bf16[128,1,2,3584]{3,2,1,0:T(2,128)(2,1)}), bf16[128,1,2,3584]{3,2,1,0:T(2,128)(2,1)S(1)}, u32[]{:S(2)}, u32[]{:S(2)}) %all-to-all-start.1) | async-done | bytes 1835040 | tf_op jit(solution)/shard_map/all_to_all | solution.py:37
  78.1 4.0 %all-to-all-start.3 = ((bf16[4,2,32768]{2,1,0:T(2,128)(2,1)}), bf16[4,2,32768]{2,1,0:T(2,128)(2,1)S(1)}, u32[]{:S(2)}, u32[]{:S(2)}) async-start(bf16[4,2,32768]{2,1,0:T(2,128)(2,1)} %reshape.148), calls=%async_computation.3 | async-start | bytes 1048576 | tf_op jit(solution)/shard_map/all_to_all | solution.py:48
  82.2 2.2 slice_bitcast_fusion.1
  84.3 3.6 %copy.51 = bf16[128,2,1792]{0,2,1:T(8,128)(2,1)} copy(bf16[128,2,1792]{2,1,0:T(2,128)(2,1)} %get-tuple-element.21) | data formatting | bytes 1835008 | tf_op jit(solution)/shard_map/slice | solution.py:55
  87.9 9.3 %all-to-all-done.3 = bf16[4,2,32768]{2,1,0:T(2,128)(2,1)S(1)} async-done(((bf16[4,2,32768]{2,1,0:T(2,128)(2,1)}), bf16[4,2,32768]{2,1,0:T(2,128)(2,1)S(1)}, u32[]{:S(2)}, u32[]{:S(2)}) %all-to-all-start.3) | async-done | bytes 524320 | tf_op jit(solution)/shard_map/all_to_all | solution.py:48
  97.3 3.5 %stack.5 = bf16[4,128,1,2,1792]{1,4,3,2,0:T(8,128)(2,1)} broadcast(bf16[128,2,1792]{0,2,1:T(8,128)(2,1)} %copy.51), dimensions={1,3,4} | broadcast | bytes 4587520 | tf_op jit(solution)/shard_map/stack | solution.py:55
  100.8 4.9 %all-to-all-start.4 = ((bf16[4,128,1,2,1792]{1,4,3,2,0:T(8,128)(2,1)}), bf16[4,128,1,2,1792]{1,4,3,2,0:T(8,128)(2,1)}, u32[]{:S(2)}, u32[]{:S(2)}) async-start(bf16[4,128,1,2,1792]{1,4,3,2,0:T(8,128)(2,1)} %stack.5), calls=%async_computation.4 | async-start | bytes 7340032 | tf_op jit(solution)/shard_map/all_to_all | solution.py:54
  105.7 2.1 copy.46
  107.9 38.6 %all-to-all-done.4 = bf16[4,128,1,2,1792]{1,4,3,2,0:T(8,128)(2,1)} async-done(((bf16[4,128,1,2,1792]{1,4,3,2,0:T(8,128)(2,1)}), bf16[4,128,1,2,1792]{1,4,3,2,0:T(8,128)(2,1)}, u32[]{:S(2)}, u32[]{:S(2)}) %all-to-all-start.4) | async-done | bytes 3670048 | tf_op jit(solution)/shard_map/all_to_all | solution.py:54
  146.4 3.4 %stack.4 = bf16[4,128,1,2,1792]{1,4,3,2,0:T(8,128)(2,1)} broadcast(bf16[128,2,1792]{0,2,1:T(8,128)(2,1)} %copy.46), dimensions={1,3,4} | broadcast | bytes 4587520 | tf_op jit(solution)/shard_map/stack | solution.py:55
  149.9 4.9 %all-to-all-start.2 = ((bf16[4,128,1,2,1792]{1,4,3,2,0:T(8,128)(2,1)}), bf16[4,128,1,2,1792]{1,4,3,2,0:T(8,128)(2,1)}, u32[]{:S(2)}, u32[]{:S(2)}) async-start(bf16[4,128,1,2,1792]{1,4,3,2,0:T(8,128)(2,1)} %stack.4), calls=%async_computation.2 | async-start | bytes 7340032 | tf_op jit(solution)/shard_map/all_to_all | solution.py:54
  154.8 6.4 %fusion.4 = bf16[256,3584]{1,0:T(8,128)(2,1)} fusion(bf16[1,1024,3584]{2,1,0:T(8,128)(2,1)} %all-gather.2.cloned.1.call-done, bf16[1,1,256,1024]{3,2,1,0:T(8,128)(2,1)S(1)} %copy-done.1), kind=kOutput, calls=%fused_computation.6 | convolution fusion | flops 1879965696 | bytes 9699328 | tf_op jit(solution)/shard_map/dot_general | solution.py:20
  161.2 4.7 %reshape.114 = bf16[128,2,3584]{2,1,0:T(2,128)(2,1)} reshape(bf16[256,3584]{1,0:T(8,128)(2,1)} %fusion.4) | data formatting | bytes 3670016 | tf_op jit(solution)/shard_map/reshape | solution.py:24
  165.9 28.9 %all-to-all-done.2 = bf16[4,128,1,2,1792]{1,4,3,2,0:T(8,128)(2,1)} async-done(((bf16[4,128,1,2,1792]{1,4,3,2,0:T(8,128)(2,1)}), bf16[4,128,1,2,1792]{1,4,3,2,0:T(8,128)(2,1)}, u32[]{:S(2)}, u32[]{:S(2)}) %all-to-all-start.2) | async-done | bytes 3670048 | tf_op jit(solution)/shard_map/all_to_all | solution.py:54
  194.8 14.3 %all-to-all-start = ((bf16[128,2,3584]{2,1,0:T(2,128)(2,1)}), bf16[128,2,3584]{2,1,0:T(2,128)(2,1)}, u32[]{:S(2)}, u32[]{:S(2)}) async-start(bf16[128,2,3584]{2,1,0:T(2,128)(2,1)} %reshape.114), calls=%async_computation | async-start | bytes 3670016 | tf_op jit(solution)/shard_map/all_to_all | solution.py:23
  212.1 3.2 %fusion.28 = bf16[256,1792]{0,1:T(8,128)(2,1)S(1)} fusion(bf16[4,128,1,2,1792]{1,4,3,2,0:T(8,128)(2,1)} %all-to-all-done.4, bf16[4,128,2,256]{3,0,2,1:T(4,128)(2,1)S(1)} %bitcast.115), kind=kOutput, calls=%fused_computation.18 | convolution fusion | flops 939982848 | bytes 5111808 | tf_op jit(solution)/shard_map/gsch,sgcd->hd/dot_general | solution.py:60
  215.3 3.2 %fusion.25 = bf16[256,1792]{0,1:T(8,128)(2,1)S(1)} fusion(bf16[4,128,1,2,1792]{1,4,3,2,0:T(8,128)(2,1)} %all-to-all-done.2, bf16[4,128,2,256]{3,0,2,1:T(4,128)(2,1)S(1)} %bitcast.116), kind=kOutput, calls=%fused_computation.17 | convolution fusion | flops 939982848 | bytes 5111808 | tf_op jit(solution)/shard_map/gsch,sgcd->hd/dot_general | solution.py:60
  218.6 2.6 copy.54
  221.2 6.5 %fusion.35 = bf16[1,1,256,1024]{3,2,1,0:T(8,128)(2,1)} fusion(bf16[256,3584]{1,0:T(8,128)(2,1)} %reshape_squeeze.6, bf16[1,1024,3584]{2,1,0:T(8,128)(2,1)} %all-gather.2.cloned.1.call-done), kind=kOutput, calls=%fused_computation.23 | convolution fusion | flops 1879310336 | bytes 9699328 | tf_op jit(solution)/shard_map/rd,hd->rh/dot_general | solution.py:45
  227.7 27.6 %all-to-all-done = bf16[128,2,3584]{2,1,0:T(2,128)(2,1)} async-done(((bf16[128,2,3584]{2,1,0:T(2,128)(2,1)}), bf16[128,2,3584]{2,1,0:T(2,128)(2,1)}, u32[]{:S(2)}, u32[]{:S(2)}) %all-to-all-start) | async-done | bytes 1835040 | tf_op jit(solution)/shard_map/all_to_all | solution.py:23
  255.2 4.1 %reshape.115 = bf16[256,3584]{1,0:T(8,128)(2,1)S(1)} reshape(bf16[128,2,3584]{2,1,0:T(2,128)(2,1)} %all-to-all-done) | data formatting | bytes 3670016 | tf_op jit(solution)/shard_map/reshape | solution.py:26
  (46 shorter events, 12.2 us)
Async XLA Ops:
  7.2 0.8 copy-start.3
  7.2 1.0 copy-start.4
  7.2 1.7 copy-start.2
  7.2 147.6 %all-gather.2.cloned.1.call-start = ((), (), s32[]{:S(2)}) async-start(), calls=%async_computation.5 | async-start | bytes 9175040 | tf_op jit(solution)/shard_map/all_gather | solution.py:19
  13.1 18.6 %copy-start = (bf16[1,1,256,1024]{3,2,1,0:T(8,128)(2,1)S(1)}, bf16[1,1,256,1024]{3,2,1,0:T(8,128)(2,1)}, u32[]{:S(2)}) copy-start(bf16[1,1,256,1024]{3,2,1,0:T(8,128)(2,1)} %param.5) | copy-start | bytes 1572868
  13.1 65.0 %all-to-all-start.1 = ((bf16[128,1,2,3584]{3,2,1,0:T(2,128)(2,1)}), bf16[128,1,2,3584]{3,2,1,0:T(2,128)(2,1)S(1)}, u32[]{:S(2)}, u32[]{:S(2)}) async-start(bf16[128,1,2,3584]{3,2,1,0:T(2,128)(2,1)} %bitcast.111), calls=%async_computation.1 | async-start | bytes 3670016 | tf_op jit(solution)/shard_map/all_to_all | solution.py:37
  78.1 19.1 %all-to-all-start.3 = ((bf16[4,2,32768]{2,1,0:T(2,128)(2,1)}), bf16[4,2,32768]{2,1,0:T(2,128)(2,1)S(1)}, u32[]{:S(2)}, u32[]{:S(2)}) async-start(bf16[4,2,32768]{2,1,0:T(2,128)(2,1)} %reshape.148), calls=%async_computation.3 | async-start | bytes 1048576 | tf_op jit(solution)/shard_map/all_to_all | solution.py:48
  100.8 45.6 %all-to-all-start.4 = ((bf16[4,128,1,2,1792]{1,4,3,2,0:T(8,128)(2,1)}), bf16[4,128,1,2,1792]{1,4,3,2,0:T(8,128)(2,1)}, u32[]{:S(2)}, u32[]{:S(2)}) async-start(bf16[4,128,1,2,1792]{1,4,3,2,0:T(8,128)(2,1)} %stack.5), calls=%async_computation.4 | async-start | bytes 7340032 | tf_op jit(solution)/shard_map/all_to_all | solution.py:54
  149.9 4.9 %copy-start.1 = (bf16[1,1,256,1024]{3,2,1,0:T(8,128)(2,1)S(1)}, bf16[1,1,256,1024]{3,2,1,0:T(8,128)(2,1)}, u32[]{:S(2)}) copy-start(bf16[1,1,256,1024]{3,2,1,0:T(8,128)(2,1)} %param.5) | copy-start | bytes 1572868
  149.9 44.9 %all-to-all-start.2 = ((bf16[4,128,1,2,1792]{1,4,3,2,0:T(8,128)(2,1)}), bf16[4,128,1,2,1792]{1,4,3,2,0:T(8,128)(2,1)}, u32[]{:S(2)}, u32[]{:S(2)}) async-start(bf16[4,128,1,2,1792]{1,4,3,2,0:T(8,128)(2,1)} %stack.4), calls=%async_computation.2 | async-start | bytes 7340032 | tf_op jit(solution)/shard_map/all_to_all | solution.py:54
  194.8 60.4 %all-to-all-start = ((bf16[128,2,3584]{2,1,0:T(2,128)(2,1)}), bf16[128,2,3584]{2,1,0:T(2,128)(2,1)}, u32[]{:S(2)}, u32[]{:S(2)}) async-start(bf16[128,2,3584]{2,1,0:T(2,128)(2,1)} %reshape.114), calls=%async_computation | async-start | bytes 3670016 | tf_op jit(solution)/shard_map/all_to_all | solution.py:23
Sparse Core Ops, SparseCore 0:
  10.1 90.5 all-gather.1
